TPU v7x, 128 devices: a whole 4x4x4 slice. The times are simulated.
128 devices in a mesh: grp: 4 (over y), cand: 32 (over x, z, core).
Axes of the slice: x: 4, y: 4, z: 4, core: 2. Of those that a mesh axis runs over, the one named last changes fastest.
Arguments:
- node_emb: bfloat16 [32, 512, 512], P('cand'), may hold values from -6 to 6
- rel_emb: float32 [900, 512], P('grp'), may hold values from -6 to 6
- w_in: bfloat16 [512, 512], replicated, may hold values from -0.25 to 0.25
- w_self: bfloat16 [512, 512], replicated, may hold values from -1 to 1
- rel_score: float32 [900, 512], replicated, may hold values from -7 to 7
- mirror_blocks: int32 [4, 32, 32, 1], P('grp', 'cand'), may hold values from 0 to 3
- adj_values: bfloat16 [4, 32, 192, 128, 128], P('grp', 'cand'), may hold values from -0.0390625 to 0.0390625
- adj_source: int32 [4, 32, 192], P('grp', 'cand'), may hold values from 0 to 31
- adj_target: int32 [4, 32, 192], P('grp', 'cand'), may hold values from 0 to 3
- adj_relation: int32 [4, 32, 192], P('grp', 'cand'), may hold values from 0 to 224
- live_blocks: int32 [4, 32], P('grp', 'cand'), may hold values from 48 to 192, as said below
- query_head: int32 [1024], replicated, may hold values from 0 to 16383
- query_rel: int32 [1024], replicated, may hold values from 0 to 899
- allowed: int32 [1024, 8], replicated, may hold values from 0 to 127, as said below
- true_tail: int32 [1024], replicated, may hold values from 0 to 16383, as said below
Outputs:
- h_out: bfloat16 [32, 512, 512], P('cand', 'grp')
- loss: float32 [1024], replicated
- grad_h: float32 [32, 512, 512], P('cand', 'grp')
- grad_rel: float32 [900, 512], P('grp')
- grad_w_in: float32 [512, 512], replicated
- grad_w_self: float32 [512, 512], replicated
Inputs may be any that keep to these rules, and one draw needn't show every extreme that they name: `live_blocks`: blocks from this count on are padding; on some device all 192 blocks are live. `allowed`: ids of blocks of 128 concepts; a query may name a block twice. `true_tail`: lies in one of the query's allowed blocks.
All inputs are finite; a program needn't handle non-finite values.
Results may differ from a plain program's by a relative error of at most 0.011.
Values may be sent and summed in bfloat16 or wider, within the bound.
A program may use at most 128 MiB of HBM per device.

v0:
```python
import math
import jax
import jax.numpy as jnp
from jax import lax
from jax.sharding import PartitionSpec as P

NEG_FILL = -1e30
HIGH = lax.Precision.HIGHEST


def body(
    node_emb,
    rel_emb,
    w_in,
    w_self,
    rel_score,
    mirror_blocks,
    adj_values,
    adj_source,
    adj_target,
    adj_relation,
    live_blocks,
    query_head,
    query_rel,
    allowed,
    true_tail,
):
    cand_count = lax.axis_size("cand")
    grp_count = lax.axis_size("grp")
    grp_index = lax.axis_index("grp")
    cand_index = lax.axis_index("cand")
    nodes = node_emb[0]
    node_rows, feature_dim = nodes.shape
    block_rows = adj_values.shape[-1]
    tile_count = node_rows // block_rows
    share_rows = node_rows // grp_count
    wanted = mirror_blocks[0, 0]
    slot_count = wanted.shape[1]
    mirror_count = cand_count * slot_count
    requested = lax.all_to_all(wanted, "cand", split_axis=0, concat_axis=0, tiled=True)
    everything = lax.all_gather(node_emb, "cand", axis=0, tiled=True)
    everything = everything.reshape(cand_count * tile_count, block_rows, feature_dim)
    owners = jnp.arange(cand_count, dtype=jnp.int32)[:, None] * tile_count
    mirrors = jnp.take(everything, (owners + wanted).reshape(-1), axis=0)
    tile_values = adj_values[0, 0]
    block_count = tile_values.shape[0]
    stride = math.gcd(block_count, 16)
    turns = block_count // stride
    live_mask = (jnp.arange(block_count, dtype=jnp.int32) < live_blocks[0, 0]).astype(jnp.float32)
    packed = (
        tile_values.reshape(turns, stride, block_rows, block_rows),
        adj_source[0, 0].reshape(turns, stride),
        adj_target[0, 0].reshape(turns, stride),
        adj_relation[0, 0].reshape(turns, stride),
        live_mask.reshape(turns, stride),
    )

    def forward_turn(partial_value, inputs_now):
        values_now, source_now, target_now, relation_now, live_now = inputs_now
        composed = (
            jnp.take(mirrors, source_now, axis=0).astype(jnp.float32)
            - jnp.take(rel_emb, relation_now, axis=0)[:, None, :]
        ).astype(jnp.bfloat16)
        messages = jnp.einsum(
            "bij,bjd->bid", values_now, composed, preferred_element_type=jnp.float32
        )
        messages = messages * live_now[:, None, None]
        return (partial_value.at[target_now].add(messages), None)

    partial_value, ignored = lax.scan(
        forward_turn, jnp.zeros((tile_count, block_rows, feature_dim), jnp.float32), packed
    )
    aggregate = lax.psum_scatter(
        partial_value.reshape(node_rows, feature_dim), "grp", scatter_dimension=0, tiled=True
    )
    aggregate_bf = aggregate.astype(jnp.bfloat16)
    own_rows = lax.dynamic_slice_in_dim(nodes, grp_index * share_rows, share_rows, 0)
    pre_act = jnp.dot(aggregate_bf, w_in, preferred_element_type=jnp.float32) + jnp.dot(
        own_rows, w_self, preferred_element_type=jnp.float32
    )
    activated = jnp.tanh(pre_act)
    h_new = activated.astype(jnp.bfloat16)
    first_row = cand_index * node_rows + grp_index * share_rows
    row_ids = first_row + jnp.arange(share_rows, dtype=jnp.int32)
    head_pick = query_head[:, None] == row_ids[None, :]
    head_part = jnp.dot(head_pick.astype(jnp.bfloat16), h_new, preferred_element_type=jnp.float32)
    heads = lax.psum(head_part, ("grp", "cand"))
    queries = heads + jnp.take(rel_score, query_rel, axis=0)
    cand_rows = h_new.astype(jnp.float32)
    scale = feature_dim ** (-0.5)
    cross = jnp.dot(queries, cand_rows.T, precision=HIGH)
    scores = -scale * (
        jnp.sum(queries * queries, axis=1)[:, None]
        + jnp.sum(cand_rows * cand_rows, axis=1)[None, :]
        - 2.0 * cross
    )
    block_ids = first_row // block_rows + jnp.arange(share_rows // block_rows, dtype=jnp.int32)
    block_ok = jnp.any(allowed[:, :, None] == block_ids[None, None, :], axis=1)
    allowed_mask = jnp.repeat(block_ok, block_rows, axis=1)
    tail_pick = true_tail[:, None] == row_ids[None, :]
    truth_part = jnp.sum(jnp.where(tail_pick, scores, 0.0), axis=1)
    local_max = jnp.max(jnp.where(allowed_mask, scores, NEG_FILL), axis=1)
    row_max = lax.pmax(local_max, ("grp", "cand"))
    local_total = jnp.sum(
        jnp.exp(jnp.where(allowed_mask, scores - row_max[:, None], NEG_FILL)), axis=1
    )
    row_total, truth = lax.psum((local_total, truth_part), ("grp", "cand"))
    log_norm = row_max + jnp.log(row_total)
    loss = log_norm - truth
    prob = jnp.exp(jnp.where(allowed_mask, scores - log_norm[:, None], NEG_FILL))
    grad_score = (prob - tail_pick.astype(jnp.float32)) / query_head.shape[0]
    query_part = (
        2.0
        * scale
        * (
            jnp.dot(grad_score, cand_rows, precision=HIGH)
            - queries * jnp.sum(grad_score, axis=1)[:, None]
        )
    )
    query_grad = lax.psum(query_part, ("grp", "cand"))
    cand_grad = (
        2.0
        * scale
        * (
            jnp.dot(grad_score.T, queries, precision=HIGH)
            - cand_rows * jnp.sum(grad_score, axis=0)[:, None]
        )
    )
    row_grad = cand_grad + jnp.dot(head_pick.astype(jnp.float32).T, query_grad, precision=HIGH)
    pre_grad = (row_grad * (1.0 - activated * activated)).astype(jnp.bfloat16)
    grad_w_in, grad_w_self = lax.psum(
        (
            jnp.dot(aggregate_bf.T, pre_grad, preferred_element_type=jnp.float32),
            jnp.dot(own_rows.T, pre_grad, preferred_element_type=jnp.float32),
        ),
        ("grp", "cand"),
    )
    agg_grad = jnp.dot(pre_grad, w_in.T, preferred_element_type=jnp.float32).astype(jnp.bfloat16)
    agg_tiles = lax.all_gather(agg_grad, "grp", axis=0, tiled=True).reshape(
        tile_count, block_rows, feature_dim
    )

    def backward_turn(carry, inputs_now):
        mirror_grad, relation_grad = carry
        values_now, source_now, target_now, relation_now, live_now = inputs_now
        composed_grad = jnp.einsum(
            "bij,bid->bjd",
            values_now,
            jnp.take(agg_tiles, target_now, axis=0),
            preferred_element_type=jnp.float32,
        )
        composed_grad = composed_grad * live_now[:, None, None]
        mirror_grad = mirror_grad.at[source_now].add(composed_grad)
        relation_grad = relation_grad.at[relation_now].add(-jnp.sum(composed_grad, axis=1))
        return ((mirror_grad, relation_grad), None)

    start = (
        jnp.zeros((mirror_count, block_rows, feature_dim), jnp.float32),
        jnp.zeros(rel_emb.shape, jnp.float32),
    )
    (mirror_grad, relation_grad), ignored = lax.scan(backward_turn, start, packed)
    grad_rel = lax.psum(relation_grad, "cand")
    returned = lax.all_to_all(
        mirror_grad.reshape(cand_count, slot_count, block_rows, feature_dim).astype(jnp.bfloat16),
        "cand",
        split_axis=0,
        concat_axis=0,
        tiled=True,
    ).astype(jnp.float32)
    owned = (
        jnp.zeros((tile_count, block_rows, feature_dim), jnp.float32)
        .at[requested.reshape(-1)]
        .add(returned.reshape(mirror_count, block_rows, feature_dim))
    )
    node_grad = lax.psum_scatter(
        owned.reshape(node_rows, feature_dim).astype(jnp.bfloat16),
        "grp",
        scatter_dimension=0,
        tiled=True,
    ).astype(jnp.float32)
    node_grad = node_grad + jnp.dot(pre_grad, w_self.T, preferred_element_type=jnp.float32)
    return (h_new[None], loss, node_grad[None], grad_rel, grad_w_in, grad_w_self)


def solution(mesh):
    return jax.shard_map(
        body,
        mesh=mesh,
        in_specs=(
            P("cand", None, None),
            P("grp", None),
            P(),
            P(),
            P(),
            P("grp", "cand", None, None),
            P("grp", "cand", None, None, None),
            P("grp", "cand", None),
            P("grp", "cand", None),
            P("grp", "cand", None),
            P("grp", "cand"),
            P(),
            P(),
            P(),
            P(),
        ),
        out_specs=(P("cand", "grp", None), P(), P("cand", "grp", None), P("grp", None), P(), P()),
        check_vma=False,
    )
```

profile of v0, /device:TPU:1, one launch (start us, length us, event | category | flops | bytes accessed | tf_op | source)
XLA Modules:
  0.0 1358.5 jit_solution(7435921861001893714)
XLA Ops:
  14.8 71.8 %all-gather.2.cloned.1.call-done = bf16[32,512,512]{2,1,0:T(8,128)(2,1)} async-done(((bf16[1,512,512]{2,1,0:T(8,128)(2,1)}), bf16[32,512,512]{2,1,0:T(8,128)(2,1)}) %all-gather.2.cloned.1.call-update) | async-done | bytes 16777232 | tf_op jit(solution)/shard_map/all_gather | solution.py:41
  86.6 8.5 gather_fusion.3
  95.1 4.6 broadcast_select_fusion.1
  99.8 187.6 %while.22 = (s32[]{:T(128)}, f32[4,128,512]{2,1,0:T(8,128)S(1)}, s32[12,16]{1,0:T(8,128)S(1)}, bf16[12,16,128,128]{3,2,1,0:T(8,128)(2,1)}, s32[12,16]{1,0:T(8,12...) while((s32[]{:T(128)}, f32[4,128,512]{2,1,0:T(8,128)S(1)}, ...), condition=%wide.region_2.3_spmd, body=%wide.region_0.0_spmd.sunk | while | flops 274737504 | bytes 23766708 | solution.py:70
  109.4 6.1 scatter_fusion
  120.4 4.6 convolution_multiply_fusion.4
  125.0 6.1 scatter_fusion
  140.6 6.1 scatter_fusion
  151.7 4.6 convolution_multiply_fusion.4
  156.3 6.1 scatter_fusion
  171.9 6.1 scatter_fusion
  187.5 6.1 scatter_fusion
  203.1 6.1 scatter_fusion
  218.8 6.1 scatter_fusion
  234.4 6.1 scatter_fusion
  250.0 6.1 scatter_fusion
  265.7 6.1 scatter_fusion
  281.3 6.1 scatter_fusion
  288.5 21.3 %reduce-scatter.3.cloned.1.call-done = f32[128,512]{1,0:T(8,128)} async-done(((f32[512,512]{1,0:T(8,128)}), f32[128,512]{1,0:T(8,128)}) %reduce-scatter.3.cloned.1.call-update) | async-done | bytes 262160 | tf_op jit(solution)/shard_map/reduce_scatter | solution.py:73
  314.4 4.9 gather_fusion.4
  319.4 147.5 %all-reduce.6.cloned.1.call-done = f32[1024,512]{1,0:T(8,128)} async-done(((f32[1024,512]{1,0:T(8,128)}), f32[1024,512]{1,0:T(8,128)}) %all-reduce.6.cloned.1.call-update) | async-done | bytes 2097168 | tf_op jit(solution)/shard_map/psum | solution.py:87
  472.4 63.8 %pmax.7 = f32[1024]{0:T(1024)S(1)} all-reduce(f32[1024]{0:T(1024)S(1)} %get-tuple-element.185), channel_id=1, replica_groups=mesh['grp'=4,'cand'=32] {'grp','cand'}, use_global_device_ids=true, to_apply=%region_9.10 | all-reduce | flops 1024 | bytes 8192 | tf_op jit(solution)/shard_map/pmax | solution.py:103
  536.3 63.8 %psum.50 = f32[1024]{0:T(1024)S(1)} all-reduce(f32[1024]{0:T(1024)S(1)} %exponential_reduce_fusion), channel_id=1, replica_groups=mesh['grp'=4,'cand'=32] {'grp','cand'}, use_global_device_ids=true, to_apply=%region_11.12 | all-reduce | flops 1024 | bytes 8192 | tf_op jit(solution)/shard_map/psum | solution.py:107
  605.9 4.7 all-to-all-start
  610.6 8.6 copy.26
  622.2 130.2 %all-reduce.8.cloned.1.call-done = f32[1024,512]{1,0:T(8,128)} async-done(((f32[1024,512]{1,0:T(8,128)}), f32[1024,512]{1,0:T(8,128)}) %all-reduce.8.cloned.1.call-update) | async-done | bytes 2097168 | tf_op jit(solution)/shard_map/psum | solution.py:120
  755.2 10.5 all_gather.7
  770.0 204.7 %while.23 = (s32[]{:T(128)}, f32[32,128,512]{2,1,0:T(8,128)}, f32[225,512]{1,0:T(8,128)S(1)}, s32[12,16]{1,0:T(8,128)S(1)}, bf16[12,16,128,128]{2,3,1,0:T(8,128)...) while((s32[]{:T(128)}, f32[32,128,512]{2,1,0:T(8,128)}, ...), condition=%wide.region_21.22_spmd, body=%wide.region_17.21_spmd.sunk | while | flops 272639232 | bytes 24124884 | solution.py:161
  776.6 9.7 scatter_fusion.1
  793.8 9.5 scatter_fusion.1
  810.7 9.6 scatter_fusion.1
  827.8 9.7 scatter_fusion.1
  845.0 9.6 scatter_fusion.1
  862.0 9.8 scatter_fusion.1
  879.3 9.5 scatter_fusion.1
  896.2 9.7 scatter_fusion.1
  913.3 9.6 scatter_fusion.1
  930.3 9.5 scatter_fusion.1
  947.3 9.6 scatter_fusion.1
  964.3 9.5 scatter_fusion.1
  974.7 6.1 convert_bitcast_fusion
  980.9 8.8 all-to-all-start.1
  990.4 51.4 %all-to-all-done.1 = bf16[32,1,128,512]{3,2,1,0:T(8,128)(2,1)} async-done(((bf16[32,1,128,512]{3,2,1,0:T(8,128)(2,1)}), bf16[32,1,128,512]{3,2,1,0:T(8,128)(2,1)}, u32[]{:S(2)}, u32[]{:S(2)}) %all-to-all-start.1) | async-done | bytes 4194336 | tf_op jit(solution)/shard_map/all_to_all | solution.py:163
  1041.8 6.6 bitcast_convert_fusion
  1048.4 11.7 scatter_fusion.2
  1065.2 65.0 %psum.51 = f32[1024]{0:T(1024)S(1)} all-reduce(f32[1024]{0:T(1024)S(1)} %get-tuple-element.133), channel_id=1, replica_groups=mesh['grp'=4,'cand'=32] {'grp','cand'}, use_global_device_ids=true, to_apply=%region_13.14 | all-reduce | flops 1024 | bytes 8192 | tf_op jit(solution)/shard_map/psum | solution.py:107
  1132.7 57.1 %all-reduce.10.cloned.1.call-done = f32[225,512]{1,0:T(8,128)} async-done(((f32[225,512]{1,0:T(8,128)}), f32[225,512]{1,0:T(8,128)}) %all-reduce.10.cloned.1.call-update) | async-done | bytes 460816 | tf_op jit(solution)/shard_map/psum | solution.py:162
  1189.8 156.6 %all-reduce.12.cloned.1.call-done = (f32[512,512]{1,0:T(8,128)}, f32[512,512]{1,0:T(8,128)}) async-done(((f32[512,512]{1,0:T(8,128)}, f32[512,512]{1,0:T(8,128)}), (f32[512,512]{1,0:T(8,128)}, f32[512,512]{1,0:T(8,128)})) %all-reduce.12.cloned.1.call-update) | async-done | bytes 2097168 | tf_op jit(solution)/shard_map/psum | solution.py:131
  (304 shorter events, 241.0 us)
Async XLA Ops:
  7.2 307.2 %copy-start = (f32[900,512]{1,0:T(8,128)S(1)}, f32[900,512]{1,0:T(8,128)}, u32[]{:S(2)}) copy-start(f32[900,512]{1,0:T(8,128)} %param.23) | copy-start | bytes 5529604
  7.2 79.4 %all-gather.2.cloned.1.call-start = ((), (), s32[]{:S(2)}) async-start(), calls=%async_computation.4 | async-start | bytes 17301504 | tf_op jit(solution)/shard_map/all_gather | solution.py:41
  7.9 301.9 %reduce-scatter.3.cloned.1.call-start = ((), (), s32[]{:S(2)}) async-start(), calls=%async_computation.5 | async-start | bytes 1310720 | tf_op jit(solution)/shard_map/reduce_scatter | solution.py:73
  95.1 4.8 copy-start.4
  287.4 1.0 copy-start.2
  287.4 23.7 %copy-start.7 = (bf16[512,512]{1,0:T(8,128)(2,1)S(1)}, bf16[512,512]{1,0:T(8,128)(2,1)}, u32[]{:S(2)}) copy-start(bf16[512,512]{1,0:T(8,128)(2,1)} %param.22) | copy-start | bytes 1572868
  287.4 25.0 %copy-start.13 = (s32[1024]{0:T(1024)S(1)}, s32[1024]{0:T(1024)}, u32[]{:S(2)}) copy-start(s32[1024]{0:T(1024)} %param.30) | copy-start | bytes 12292
  288.4 178.4 %all-reduce.6.cloned.1.call-start = ((), (), s32[]{:S(2)}) async-start(), calls=%async_computation.6 | async-start | bytes 4194304 | tf_op jit(solution)/shard_map/psum | solution.py:87
  312.4 306.8 %copy-start.5 = (bf16[128,512]{1,0:T(8,128)(2,1)}, bf16[128,512]{1,0:T(8,128)(2,1)S(1)}, u32[]{:S(2)}) copy-start(bf16[128,512]{1,0:T(8,128)(2,1)S(1)} %get-tuple-element.175) | copy-start | bytes 393220
  312.4 2.0 copy-start.14
  314.3 438.1 %all-reduce.8.cloned.1.call-start = ((), (), s32[]{:S(2)}) async-start(), calls=%async_computation.7 | async-start | bytes 4194304 | tf_op jit(solution)/shard_map/psum | solution.py:120
  314.4 4.9 copy-start.12
  469.7 1.3 copy-start.3
  469.7 130.3 %copy-start.11 = (s32[1024]{0:T(1024)S(1)}, s32[1024]{0:T(1024)}, u32[]{:S(2)}) copy-start(s32[1024]{0:T(1024)} %param.33) | copy-start | bytes 12292
  604.6 0.7 copy-start.15
  605.9 374.9 %all-to-all-start = ((s32[32,1,1]{2,1,0:T(1,128)}), s32[32,1,1]{2,1,0:T(1,128)S(1)}, u32[]{:S(2)}, u32[]{:S(2)}) async-start(s32[32,1,1]{2,1,0:T(1,128)} %copy.28), calls=%async_computation.1 | async-start | bytes 32768 | tf_op jit(solution)/shard_map/all_to_all | solution.py:40
  622.2 132.7 %copy-start.6 = (bf16[512,512]{1,0:T(8,128)(2,1)S(1)}, bf16[512,512]{1,0:T(8,128)(2,1)}, u32[]{:S(2)}) copy-start(bf16[512,512]{1,0:T(8,128)(2,1)} %param.21) | copy-start | bytes 1572868
  974.7 6.2 copy-start.8
  980.9 60.9 %all-to-all-start.1 = ((bf16[32,1,128,512]{3,2,1,0:T(8,128)(2,1)}), bf16[32,1,128,512]{3,2,1,0:T(8,128)(2,1)}, u32[]{:S(2)}, u32[]{:S(2)}) async-start(bf16[32,1,128,512]{3,2,1,0:T(8,128)(2,1)} %convert_bitcast_fusion), calls=%async_computation.2 | async-start | bytes 8388608 | tf_op jit(solution)/shard_map/all_to_all | solution.py:163
  989.7 141.1 %reduce-scatter.5.cloned.1.call-start = ((), (), s32[]{:S(2)}) async-start(), calls=%async_computation.8 | async-start | bytes 655360 | tf_op jit(solution)/shard_map/reduce_scatter | solution.py:175
  1060.1 1.5 copy-start.10
  1061.0 128.7 %all-reduce.10.cloned.1.call-start = ((), (), s32[]{:S(2)}) async-start(), calls=%async_computation.9 | async-start | bytes 950272 | tf_op jit(solution)/shard_map/psum | solution.py:162
  1061.6 284.8 %all-reduce.12.cloned.1.call-start = ((), (), s32[]{:S(2)}) async-start(), calls=%async_computation.10 | async-start | bytes 4194304 | tf_op jit(solution)/shard_map/psum | solution.py:131
  1346.4 4.2 copy-start.9
  1346.4 5.2 copy-start.1
Sparse Core Ops, SparseCore 0:
  10.3 76.2 all-gather.1
  288.5 21.2 reduce-scatter.2
  314.7 152.1 all-reduce.5
  604.7 147.6 all-reduce.7
  1061.2 19.2 reduce-scatter.4
  1084.1 105.5 all-reduce.9
  1195.4 150.9 all-reduce.11
where the time goes:
time: 1360 us
  waiting for transfers between devices  637 us (47%)
  other arithmetic  241 us (18%)
  blocking collectives  203 us (15%)
  matrix products  130 us (10%)
  local copies, waits for them, and re-layouts  117 us (9%)
  between operations  15.1 us (1%)
  starting transfers between devices  13.8 us (1%)
    psum x1, waiting for transfers between devices, body(): lax.psum((jnp.dot(aggregate_bf.T, pre_grad, preferred_element_type=jnp.fl...  157 us
    psum x1, waiting for transfers between devices, body(): heads = lax.psum(head_part, ('grp', 'cand'))  147 us
    psum x1, waiting for transfers between devices, body(): query_grad = lax.psum(query_part, ('grp', 'cand'))  130 us
    psum x2, blocking collectives, body(): row_total, truth = lax.psum((local_total, truth_part), ('grp', 'cand'))  129 us
    scatter-add x12, other arithmetic, backward_turn(): mirror_grad = mirror_grad.at[source_now].add(composed_grad)  115 us
    scatter-add x12, other arithmetic, forward_turn(): return (partial_value.at[target_now].add(messages), None)  73.3 us
    all_gather x1, waiting for transfers between devices, body(): everything = lax.all_gather(node_emb, 'cand', axis=0, tiled=True)  71.8 us
    pmax x1, blocking collectives, body(): row_max = lax.pmax(local_max, ('grp', 'cand'))  63.8 us
  transfers between devices with their start and end apart: 9, of which 7 were waited for; matrix products, arithmetic and copies ran while one was open for 18% of the time, Pallas kernels for 0%

commit v1 on v0

--- a/solution.py
+++ b/solution.py
@@ -159,7 +159,11 @@
         jnp.zeros(rel_emb.shape, jnp.float32),
     )
     (mirror_grad, relation_grad), ignored = lax.scan(backward_turn, start, packed)
-    grad_rel = lax.psum(relation_grad, "cand")
+    grad_rel = relation_grad
+    for hop in (1, 2, 4, 8, 16):
+        grad_rel = grad_rel + lax.ppermute(
+            grad_rel, "cand", [(dev, dev ^ hop) for dev in range(32)]
+        )
     returned = lax.all_to_all(
         mirror_grad.reshape(cand_count, slot_count, block_rows, feature_dim).astype(jnp.bfloat16),
         "cand",

time: 1360 us -> 1250 us (0.919)
  waiting for transfers between devices: 637 us -> 520 us
    psum x1, waiting for transfers between devices: 157 us -> 78.7 us  [body(): lax.psum((jnp.dot(aggregate_bf.T, pre_grad, preferred_element_type=jnp.fl...]
    psum x1 -> x0, waiting for transfers between devices: 57.1 us -> none  [body(): grad_rel = lax.psum(relation_grad, 'cand')]
    ppermute x0 -> x5, waiting for transfers between devices: none -> 21 us  [body(): lax.ppermute(grad_rel, 'cand', [(dev, dev ^ hop) for dev in range(32)])]
  transfers between devices with their start and end apart: 9 -> 13, of which waited for: 7 -> 9; matrix products, arithmetic and copies ran while one was open for 18% -> 21% of each run, Pallas kernels for 0% -> 0%
where the time goes in v1:
time: 1250 us
  waiting for transfers between devices  520 us (42%)
  other arithmetic  241 us (19%)
  blocking collectives  206 us (16%)
  matrix products  130 us (10%)
  local copies, waits for them, and re-layouts  116 us (9%)
  starting transfers between devices  19 us (2%)
  between operations  15.1 us (1%)
    psum x1, waiting for transfers between devices, body(): heads = lax.psum(head_part, ('grp', 'cand'))  147 us
    psum x2, blocking collectives, body(): row_total, truth = lax.psum((local_total, truth_part), ('grp', 'cand'))  132 us
    psum x1, waiting for transfers between devices, body(): query_grad = lax.psum(query_part, ('grp', 'cand'))  130 us
    scatter-add x12, other arithmetic, backward_turn(): mirror_grad = mirror_grad.at[source_now].add(composed_grad)  115 us
    psum x1, waiting for transfers between devices, body(): lax.psum((jnp.dot(aggregate_bf.T, pre_grad, preferred_element_type=jnp.fl...  78.7 us
    scatter-add x12, other arithmetic, forward_turn(): return (partial_value.at[target_now].add(messages), None)  73.3 us
    all_gather x1, waiting for transfers between devices, body(): everything = lax.all_gather(node_emb, 'cand', axis=0, tiled=True)  71.8 us
    pmax x1, blocking collectives, body(): row_max = lax.pmax(local_max, ('grp', 'cand'))  63.8 us
  transfers between devices with their start and end apart: 13, of which 9 were waited for; matrix products, arithmetic and copies ran while one was open for 21% of the time, Pallas kernels for 0%

profile of v1, /device:TPU:1, one launch (start us, length us, event | category | flops | bytes accessed | tf_op | source)
XLA Modules:
  0.0 1248.6 jit_solution(9790075393450332530)
XLA Ops:
  14.8 71.8 %all-gather.2.cloned.1.call-done = bf16[32,512,512]{2,1,0:T(8,128)(2,1)} async-done(((bf16[1,512,512]{2,1,0:T(8,128)(2,1)}), bf16[32,512,512]{2,1,0:T(8,128)(2,1)}) %all-gather.2.cloned.1.call-update) | async-done | bytes 16777232 | tf_op jit(solution)/shard_map/all_gather | solution.py:41
  86.6 8.5 gather_fusion.3
  95.1 4.6 broadcast_select_fusion.1
  99.8 187.6 %while.22 = (s32[]{:T(128)}, f32[4,128,512]{2,1,0:T(8,128)S(1)}, s32[12,16]{1,0:T(8,128)S(1)}, bf16[12,16,128,128]{3,2,1,0:T(8,128)(2,1)}, s32[12,16]{1,0:T(8,12...) while((s32[]{:T(128)}, f32[4,128,512]{2,1,0:T(8,128)S(1)}, ...), condition=%wide.region_2.3_spmd, body=%wide.region_0.0_spmd.sunk | while | flops 274737504 | bytes 23766708 | solution.py:70
  109.4 6.1 scatter_fusion
  125.0 6.1 scatter_fusion
  140.6 6.1 scatter_fusion
  151.7 4.6 convolution_multiply_fusion.4
  156.3 6.1 scatter_fusion
  171.9 6.1 scatter_fusion
  187.5 6.1 scatter_fusion
  203.1 6.1 scatter_fusion
  218.8 6.1 scatter_fusion
  234.4 6.1 scatter_fusion
  250.0 6.1 scatter_fusion
  265.7 6.1 scatter_fusion
  281.3 6.1 scatter_fusion
  288.5 21.3 %reduce-scatter.3.cloned.1.call-done = f32[128,512]{1,0:T(8,128)} async-done(((f32[512,512]{1,0:T(8,128)}), f32[128,512]{1,0:T(8,128)}) %reduce-scatter.3.cloned.1.call-update) | async-done | bytes 262160 | tf_op jit(solution)/shard_map/reduce_scatter | solution.py:73
  314.4 4.9 gather_fusion.4
  319.4 147.5 %all-reduce.5.cloned.1.call-done = f32[1024,512]{1,0:T(8,128)} async-done(((f32[1024,512]{1,0:T(8,128)}), f32[1024,512]{1,0:T(8,128)}) %all-reduce.5.cloned.1.call-update) | async-done | bytes 2097168 | tf_op jit(solution)/shard_map/psum | solution.py:87
  472.4 63.8 %pmax.7 = f32[1024]{0:T(1024)S(1)} all-reduce(f32[1024]{0:T(1024)S(1)} %get-tuple-element.185), channel_id=1, replica_groups=mesh['grp'=4,'cand'=32] {'grp','cand'}, use_global_device_ids=true, to_apply=%region_9.10 | all-reduce | flops 1024 | bytes 8192 | tf_op jit(solution)/shard_map/pmax | solution.py:103
  536.3 63.8 %psum.43 = f32[1024]{0:T(1024)S(1)} all-reduce(f32[1024]{0:T(1024)S(1)} %exponential_reduce_fusion), channel_id=1, replica_groups=mesh['grp'=4,'cand'=32] {'grp','cand'}, use_global_device_ids=true, to_apply=%region_11.12 | all-reduce | flops 1024 | bytes 8192 | tf_op jit(solution)/shard_map/psum | solution.py:107
  605.9 4.7 all-to-all-start
  610.7 8.6 copy.26
  622.3 130.1 %all-reduce.7.cloned.1.call-done = f32[1024,512]{1,0:T(8,128)} async-done(((f32[1024,512]{1,0:T(8,128)}), f32[1024,512]{1,0:T(8,128)}) %all-reduce.7.cloned.1.call-update) | async-done | bytes 2097168 | tf_op jit(solution)/shard_map/psum | solution.py:120
  755.2 10.5 all_gather.7
  770.1 204.6 %while.23 = (s32[]{:T(128)}, f32[32,128,512]{2,1,0:T(8,128)}, f32[225,512]{1,0:T(8,128)S(1)}, s32[12,16]{1,0:T(8,128)S(1)}, bf16[12,16,128,128]{2,3,1,0:T(8,128)...) while((s32[]{:T(128)}, f32[32,128,512]{2,1,0:T(8,128)}, ...), condition=%wide.region_21.22_spmd, body=%wide.region_17.21_spmd.sunk | while | flops 272639232 | bytes 24124884 | solution.py:161
  776.6 9.7 scatter_fusion.1
  793.8 9.5 scatter_fusion.1
  810.7 9.6 scatter_fusion.1
  827.8 9.7 scatter_fusion.1
  845.0 9.6 scatter_fusion.1
  862.1 9.8 scatter_fusion.1
  879.3 9.5 scatter_fusion.1
  896.2 9.7 scatter_fusion.1
  913.3 9.6 scatter_fusion.1
  930.4 9.5 scatter_fusion.1
  947.3 9.6 scatter_fusion.1
  964.4 9.5 scatter_fusion.1
  974.7 6.0 convert_bitcast_fusion
  980.7 8.8 all-to-all-start.1
  993.0 48.6 %all-to-all-done.1 = bf16[32,1,128,512]{3,2,1,0:T(8,128)(2,1)} async-done(((bf16[32,1,128,512]{3,2,1,0:T(8,128)(2,1)}), bf16[32,1,128,512]{3,2,1,0:T(8,128)(2,1)}, u32[]{:S(2)}, u32[]{:S(2)}) %all-to-all-start.1) | async-done | bytes 4194336 | tf_op jit(solution)/shard_map/all_to_all | solution.py:167
  1041.6 6.6 bitcast_convert_fusion
  1048.3 11.7 scatter_fusion.2
  1062.8 11.6 collective-permute-done.2
  1077.0 8.5 collective-permute-done.3
  1088.2 68.1 %psum.44 = f32[1024]{0:T(1024)S(1)} all-reduce(f32[1024]{0:T(1024)S(1)} %get-tuple-element.133), channel_id=1, replica_groups=mesh['grp'=4,'cand'=32] {'grp','cand'}, use_global_device_ids=true, to_apply=%region_13.14 | all-reduce | flops 1024 | bytes 8192 | tf_op jit(solution)/shard_map/psum | solution.py:107
  1159.7 78.7 %all-reduce.9.cloned.1.call-done = (f32[512,512]{1,0:T(8,128)}, f32[512,512]{1,0:T(8,128)}) async-done(((f32[512,512]{1,0:T(8,128)}, f32[512,512]{1,0:T(8,128)}), (f32[512,512]{1,0:T(8,128)}, f32[512,512]{1,0:T(8,128)})) %all-reduce.9.cloned.1.call-update) | async-done | bytes 2097168 | tf_op jit(solution)/shard_map/psum | solution.py:131
  (313 shorter events, 250.4 us)
Async XLA Ops:
  7.2 307.2 %copy-start = (f32[900,512]{1,0:T(8,128)S(1)}, f32[900,512]{1,0:T(8,128)}, u32[]{:S(2)}) copy-start(f32[900,512]{1,0:T(8,128)} %param.23) | copy-start | bytes 5529604
  7.2 79.4 %all-gather.2.cloned.1.call-start = ((), (), s32[]{:S(2)}) async-start(), calls=%async_computation.4 | async-start | bytes 17301504 | tf_op jit(solution)/shard_map/all_gather | solution.py:41
  7.9 301.9 %reduce-scatter.3.cloned.1.call-start = ((), (), s32[]{:S(2)}) async-start(), calls=%async_computation.5 | async-start | bytes 1310720 | tf_op jit(solution)/shard_map/reduce_scatter | solution.py:73
  95.1 4.8 copy-start.4
  287.4 1.0 copy-start.2
  287.4 23.7 %copy-start.7 = (bf16[512,512]{1,0:T(8,128)(2,1)S(1)}, bf16[512,512]{1,0:T(8,128)(2,1)}, u32[]{:S(2)}) copy-start(bf16[512,512]{1,0:T(8,128)(2,1)} %param.22) | copy-start | bytes 1572868
  287.4 25.0 %copy-start.12 = (s32[1024]{0:T(1024)S(1)}, s32[1024]{0:T(1024)}, u32[]{:S(2)}) copy-start(s32[1024]{0:T(1024)} %param.30) | copy-start | bytes 12292
  288.4 178.4 %all-reduce.5.cloned.1.call-start = ((), (), s32[]{:S(2)}) async-start(), calls=%async_computation.6 | async-start | bytes 4194304 | tf_op jit(solution)/shard_map/psum | solution.py:87
  312.4 306.8 %copy-start.5 = (bf16[128,512]{1,0:T(8,128)(2,1)}, bf16[128,512]{1,0:T(8,128)(2,1)S(1)}, u32[]{:S(2)}) copy-start(bf16[128,512]{1,0:T(8,128)(2,1)S(1)} %get-tuple-element.175) | copy-start | bytes 393220
  312.4 2.0 copy-start.13
  314.3 438.1 %all-reduce.7.cloned.1.call-start = ((), (), s32[]{:S(2)}) async-start(), calls=%async_computation.7 | async-start | bytes 4194304 | tf_op jit(solution)/shard_map/psum | solution.py:120
  314.4 4.9 copy-start.11
  469.7 1.3 copy-start.3
  469.7 130.4 %copy-start.10 = (s32[1024]{0:T(1024)S(1)}, s32[1024]{0:T(1024)}, u32[]{:S(2)}) copy-start(s32[1024]{0:T(1024)} %param.33) | copy-start | bytes 12292
  604.6 0.7 copy-start.14
  605.9 374.8 %all-to-all-start = ((s32[32,1,1]{2,1,0:T(1,128)}), s32[32,1,1]{2,1,0:T(1,128)S(1)}, u32[]{:S(2)}, u32[]{:S(2)}) async-start(s32[32,1,1]{2,1,0:T(1,128)} %copy.28), calls=%async_computation.1 | async-start | bytes 32768 | tf_op jit(solution)/shard_map/all_to_all | solution.py:40
  622.3 132.6 %copy-start.6 = (bf16[512,512]{1,0:T(8,128)(2,1)S(1)}, bf16[512,512]{1,0:T(8,128)(2,1)}, u32[]{:S(2)}) copy-start(bf16[512,512]{1,0:T(8,128)(2,1)} %param.21) | copy-start | bytes 1572868
  980.7 60.9 %all-to-all-start.1 = ((bf16[32,1,128,512]{3,2,1,0:T(8,128)(2,1)}), bf16[32,1,128,512]{3,2,1,0:T(8,128)(2,1)}, u32[]{:S(2)}, u32[]{:S(2)}) async-start(bf16[32,1,128,512]{3,2,1,0:T(8,128)(2,1)} %convert_bitcast_fusion), calls=%async_computation.2 | async-start | bytes 8388608 | tf_op jit(solution)/shard_map/all_to_all | solution.py:167
  989.5 168.3 %reduce-scatter.5.cloned.1.call-start = ((), (), s32[]{:S(2)}) async-start(), calls=%async_computation.8 | async-start | bytes 655360 | tf_op jit(solution)/shard_map/reduce_scatter | solution.py:179
  989.5 1.9 collective-permute-start
  991.5 69.4 %collective-permute-start.1 = (f32[225,512]{1,0:T(8,128)S(1)}, f32[225,512]{1,0:T(8,128)S(1)}, u32[]{:S(2)}, u32[]{:S(2)}) collective-permute-start(f32[225,512]{1,0:T(8,128)S(1)} %add.244), channel_id=1, source_target_pairs={{0,2},{1,3},{2,0},{3,1},{4,6},{5,7},{6,4},{7,5},{8,10},{9,11},{10,... | collective-permute-start | bytes 1382408 | tf_op jit(solution)/shard_map/ppermute | solution.py:164
  1060.0 1.5 copy-start.9
  1060.9 177.5 %all-reduce.9.cloned.1.call-start = ((), (), s32[]{:S(2)}) async-start(), calls=%async_computation.9 | async-start | bytes 4194304 | tf_op jit(solution)/shard_map/psum | solution.py:131
  1061.0 13.4 %collective-permute-start.2 = (f32[225,512]{1,0:T(8,128)S(1)}, f32[225,512]{1,0:T(8,128)S(1)}, u32[]{:S(2)}, u32[]{:S(2)}) collective-permute-start(f32[225,512]{1,0:T(8,128)S(1)} %add.245), channel_id=1, source_target_pairs={{0,4},{1,5},{2,6},{3,7},{4,0},{5,1},{6,2},{7,3},{8,12},{9,13},{10,... | collective-permute-start | bytes 1382408 | tf_op jit(solution)/shard_map/ppermute | solution.py:164
  1074.5 11.0 collective-permute-start.3
  1085.6 71.3 %collective-permute-start.4 = (f32[225,512]{1,0:T(8,128)S(1)}, f32[225,512]{1,0:T(8,128)S(1)}, u32[]{:S(2)}, u32[]{:S(2)}) collective-permute-start(f32[225,512]{1,0:T(8,128)S(1)} %add.247), channel_id=1, source_target_pairs={{0,16},{1,17},{2,18},{3,19},{4,20},{5,21},{6,22},{7,23},{8,24},{9,... | collective-permute-start | bytes 1382408 | tf_op jit(solution)/shard_map/ppermute | solution.py:164
  1238.4 2.4 copy-start.8
  1238.4 3.4 copy-start.1
Sparse Core Ops, SparseCore 0:
  10.3 76.2 all-gather.1
  288.5 21.2 reduce-scatter.2
  314.7 152.1 all-reduce.4
  604.7 147.6 all-reduce.6
  1061.0 18.4 reduce-scatter.4
  1084.9 153.3 all-reduce.8
